TPU v7x, 128 devices: a whole 4x4x4 slice. The times are simulated.
128 devices in a mesh: gx: 8 (over y_lo, x), gy: 16 (over y_hi, z, core).
Axes of the slice: x: 4, y: 4 (y_hi: 2, y_lo: 2; y = y_hi * 2 + y_lo), z: 4, core: 2. Of those that a mesh axis runs over, the one named last changes fastest.
Arguments:
- patches: bfloat16 [1024, 6144], P('gy', 'gx'), may hold values from -2000 to 2000
- norm_gain: float32 [6144], P('gx'), may hold values from 0.5 to 1.5
- w_up: bfloat16 [6144, 24576], P('gx', 'gy'), may hold values from -0.078125 to 0.078125
- bias_up: float32 [24576], P('gy'), may hold values from -4 to 4
- w_down: bfloat16 [24576, 6144], P('gy', 'gx'), may hold values from -0.0390625 to 0.0390625
- bias_down: float32 [6144], P('gx'), may hold values from -4 to 4
- cotangent: bfloat16 [1024, 6144], P('gy', 'gx'), may hold values from -4 to 4
Outputs:
- mlp_out: bfloat16 [1024, 6144], P('gy', 'gx')
- grad_patches: bfloat16 [1024, 6144], P('gy', 'gx')
- grad_gain: float32 [6144], P('gx')
- grad_w_up: float32 [6144, 24576], P('gx', 'gy')
- grad_bias_up: float32 [24576], P('gy')
- grad_w_down: float32 [24576, 6144], P('gy', 'gx')
- grad_bias_down: float32 [6144], P('gx')
All inputs are finite; a program needn't handle non-finite values.
Results may differ from a plain program's by a relative error of at most 0.007.
Values may be sent and summed in bfloat16 or wider, within the bound.
A program may use at most 128 MiB of HBM per device.

v0:
```python
import jax
import jax.numpy as jnp
from jax import lax
from jax.sharding import PartitionSpec as P

D = 6144
epsilon = 1e-06
inv_root_two = 0.7071067811865476
inv_root_two_pi = 0.3989422804014327


def gelu_value(hidden):
    return 0.5 * hidden * (1.0 + lax.erf(hidden * inv_root_two))


def gelu_slope(hidden):
    return (
        0.5 * (1.0 + lax.erf(hidden * inv_root_two))
        + hidden * jnp.exp(-0.5 * hidden * hidden) * inv_root_two_pi
    )


def over_rows(left, right):
    return lax.dot_general(
        left, right, (((0,), (0,)), ((), ())), preferred_element_type=jnp.float32
    )


def over_cols(left, right):
    return lax.dot_general(
        left, right, (((1,), (1,)), ((), ())), preferred_element_type=jnp.float32
    )


def shards(patches, norm_gain, w_up, bias_up, w_down, bias_down, cotangent):
    values = patches.astype(jnp.float32)
    row_total, row_squares = lax.psum(
        (jnp.sum(values, axis=1), jnp.sum(values * values, axis=1)), "gx"
    )
    row_mean = (row_total / D)[:, None]
    variance = (row_squares / D)[:, None] - row_mean * row_mean
    inv_std = lax.rsqrt(variance + epsilon)
    standard = (values - row_mean) * inv_std
    normed = (standard * norm_gain).astype(jnp.bfloat16)
    partial_value = jnp.dot(
        lax.all_gather(normed, "gy", axis=0, tiled=True), w_up, preferred_element_type=jnp.float32
    )
    hidden = lax.psum(partial_value, "gx") + bias_up
    act_whole = gelu_value(hidden).astype(jnp.bfloat16)
    block = act_whole
    mlp_out = (
        lax.psum_scatter(
            jnp.dot(block, w_down, preferred_element_type=jnp.float32),
            "gy",
            scatter_dimension=0,
            tiled=True,
        )
        + bias_down
    ).astype(jnp.bfloat16)
    piece = lax.all_gather(cotangent, "gy", axis=0, tiled=True)
    weight_total = over_rows(act_whole, piece)
    act_grads = over_cols(piece, w_down)
    grad_act = lax.psum(act_grads, "gx")
    grad_whole = (grad_act * gelu_slope(hidden)).astype(jnp.bfloat16)
    grad_bias_up = jnp.sum(grad_whole, axis=0, dtype=jnp.float32)
    grad_w_up = over_rows(lax.all_gather(normed, "gy", axis=0, tiled=True), grad_whole)
    block = grad_whole
    grad_normed = lax.psum_scatter(over_cols(block, w_up), "gy", scatter_dimension=0, tiled=True)
    grad_gain, grad_bias_down = lax.psum(
        (jnp.sum(grad_normed * standard, axis=0), jnp.sum(cotangent, axis=0, dtype=jnp.float32)),
        "gy",
    )
    scaled = grad_normed * norm_gain
    first_total, second_total = lax.psum(
        (jnp.sum(scaled, axis=1), jnp.sum(scaled * standard, axis=1)), "gx"
    )
    first_mean = (first_total / D)[:, None]
    second_mean = (second_total / D)[:, None]
    grad_patches = (inv_std * (scaled - first_mean - standard * second_mean)).astype(jnp.bfloat16)
    return (mlp_out, grad_patches, grad_gain, grad_w_up, grad_bias_up, weight_total, grad_bias_down)


def solution(mesh):
    in_specs = (
        P("gy", "gx"),
        P("gx"),
        P("gx", "gy"),
        P("gy"),
        P("gy", "gx"),
        P("gx"),
        P("gy", "gx"),
    )
    out_specs = (
        P("gy", "gx"),
        P("gy", "gx"),
        P("gx"),
        P("gx", "gy"),
        P("gy"),
        P("gy", "gx"),
        P("gx"),
    )
    return jax.shard_map(shards, mesh=mesh, in_specs=in_specs, out_specs=out_specs, check_vma=False)
```

profile of v0, /device:TPU:0, one launch (start us, length us, event | category | flops | bytes accessed | tf_op | source)
XLA Modules:
  0.0 570.0 jit_solution(7899502057630705862)
XLA Ops:
  7.2 0.0 all-gather.3.cloned.1.call-start
  7.2 1.2 convert_reduce_fusion.1
  8.4 19.8 %all-reduce.2 = (f32[64]{0:T(128)S(1)}, f32[64]{0:T(128)S(1)}) all-reduce(f32[64]{0:T(128)S(1)} %get-tuple-element.11, f32[64]{0:T(128)S(1)} %get-tuple-element.10), channel_id=1, replica_groups=mesh['gx'=8,'gy'=16] {'gx'}, use_global_device_ids=true, to_apply=%region_3.0 | all-reduce | flops 128 | bytes 1024 | tf_op jit(solution)/shard_map/psum | solution.py:37
  28.2 1.6 fusion.11
  29.9 0.0 all-gather.3.cloned.1.call-update
  29.9 0.0 all-gather.5.cloned.1.call-start
  29.9 0.7 all-gather.5.cloned.1.call-update
  30.6 0.0 all-reduce.6.cloned.1.call-start
  30.7 45.4 %all-gather.3.cloned.1.call-done = bf16[1024,768]{1,0:T(8,128)(2,1)} async-done(((bf16[64,768]{1,0:T(8,128)(2,1)}), bf16[1024,768]{1,0:T(8,128)(2,1)}) %all-gather.3.cloned.1.call-update) | async-done | bytes 1572880 | tf_op jit(solution)/shard_map/all_gather | solution.py:46
  76.0 5.9 %fusion.19 = f32[1024,1536]{1,0:T(8,128)} fusion(bf16[1024,768]{1,0:T(8,128)(2,1)} %all-gather.3.cloned.1.call-done, bf16[768,1536]{1,0:T(8,128)(2,1)S(1)} %copy-done), kind=kOutput, calls=%fused_computation.32 | convolution fusion | flops 2415919104 | bytes 10223616 | tf_op jit(solution)/shard_map/dot_general | solution.py:45
  81.9 41.7 %all-gather.5.cloned.1.call-done = bf16[1024,768]{1,0:T(8,128)(2,1)} async-done(((bf16[64,768]{1,0:T(8,128)(2,1)}), bf16[1024,768]{1,0:T(8,128)(2,1)}) %all-gather.5.cloned.1.call-update) | async-done | bytes 1572880 | tf_op jit(solution)/shard_map/all_gather | solution.py:60
  123.6 7.4 %fusion.21 = f32[1024,1536]{1,0:T(8,128)} fusion(bf16[1024,768]{1,0:T(8,128)(2,1)} %all-gather.5.cloned.1.call-done, bf16[1536,768]{1,0:T(8,128)(2,1)} %param.11), kind=kOutput, calls=%fused_computation.34 | convolution fusion | flops 2415919104 | bytes 10223616 | tf_op jit(solution)/shard_map/dot_general | solution.py:30
  131.0 0.0 all-reduce.6.cloned.1.call-update
  131.0 0.0 reduce-scatter.5.cloned.1.call-start
  131.1 262.5 %all-reduce.6.cloned.1.call-done = (f32[1024,1536]{1,0:T(8,128)}, f32[1024,1536]{1,0:T(8,128)}) async-done(((f32[1024,1536]{1,0:T(8,128)}, f32[1024,1536]{1,0:T(8,128)}), (f32[1024,1536]{1,0:T(8,128)}, f32[1024,1536]{1,0:T(8,128)})) %all-reduce.6.cloned.1.call-update) | async-done | bytes 12582928 | tf_op jit(solution)/shard_map/psum | solution.py:48
  393.6 9.2 %convert_reduce_fusion = (f32[1536]{0:T(1024)}, bf16[1024,1536]{1,0:T(8,128)(2,1)S(1)}, bf16[1024,1536]{1,0:T(8,128)(2,1)}) fusion(f32[1024,1536]{1,0:T(8,128)} %get-tuple-element.19, f32[1024,1536]{1,0:T(8,128)} %get-tuple-element.18, f32[1536]{0:T(1024)S(1)} %copy-done.6), kind=kLoop, calls=%fused_computation.7 | loop fusion | flops 25164288 | bytes 18886656 | tf_op jit(solution)/shard_map/reduce_sum | solution.py:65
  402.8 1.7 copy-done.1
  404.5 4.3 fusion.22
  408.8 0.0 reduce-scatter.5.cloned.1.call-update
  408.8 0.0 reduce-scatter.3.cloned.1.call-start
  408.9 6.9 %fusion.20 = f32[1024,768]{1,0:T(8,128)} fusion(bf16[1024,1536]{1,0:T(8,128)(2,1)} %get-tuple-element.22, bf16[1536,768]{1,0:T(8,128)(2,1)} %param.11), kind=kOutput, calls=%fused_computation.33 | convolution fusion | flops 2415919104 | bytes 8650752 | tf_op jit(solution)/shard_map/dot_general | solution.py:53
  415.8 0.0 reduce-scatter.3.cloned.1.call-update
  415.8 0.9 copy-done.4
  416.7 7.5 %fusion.23 = f32[768,1536]{1,0:T(8,128)} fusion(bf16[1024,768]{1,0:T(8,128)(2,1)} %all-gather.3.cloned.1.call-done, bf16[1024,1536]{1,0:T(8,128)(2,1)} %copy-done.1), kind=kOutput, calls=%fused_computation.36 | convolution fusion | flops 2415919104 | bytes 9437184 | tf_op jit(solution)/shard_map/dot_general | solution.py:24
  424.3 4.4 fusion.24
  428.6 54.9 %reduce-scatter.5.cloned.1.call-done = f32[64,768]{1,0:T(8,128)} async-done(((f32[1024,768]{1,0:T(8,128)}), f32[64,768]{1,0:T(8,128)}) %reduce-scatter.5.cloned.1.call-update) | async-done | bytes 196624 | tf_op jit(solution)/shard_map/reduce_scatter | solution.py:68
  483.5 1.2 fusion.16
  484.7 18.7 %all-reduce.1 = (f32[64]{0:T(128)S(1)}, f32[64]{0:T(128)S(1)}) all-reduce(f32[64]{0:T(128)S(1)} %get-tuple-element.8, f32[64]{0:T(128)S(1)} %get-tuple-element.9), channel_id=1, replica_groups=mesh['gx'=8,'gy'=16] {'gx'}, use_global_device_ids=true, to_apply=%region_11.0 | all-reduce | flops 128 | bytes 1024 | tf_op jit(solution)/shard_map/psum | solution.py:74
  503.3 34.6 %all-reduce = (f32[768]{0:T(1024)}, f32[768]{0:T(1024)}) all-reduce(f32[768]{0:T(1024)S(1)} %get-tuple-element.7, f32[768]{0:T(1024)S(1)} %convert_reduce_fusion.2), channel_id=1, replica_groups=mesh['gx'=8,'gy'=16] {'gy'}, use_global_device_ids=true, to_apply=%region_13.0 | all-reduce | flops 1536 | bytes 12288 | tf_op jit(solution)/shard_map/psum | solution.py:69
  538.0 1.7 fusion.15
  539.7 22.2 %reduce-scatter.3.cloned.1.call-done = f32[64,768]{1,0:T(8,128)} async-done(((f32[1024,768]{1,0:T(8,128)}), f32[64,768]{1,0:T(8,128)}) %reduce-scatter.3.cloned.1.call-update) | async-done | bytes 196624 | tf_op jit(solution)/shard_map/reduce_scatter | solution.py:52
  561.9 1.6 add_convert_fusion
  (19 shorter events, 0.1 us)
Async XLA Ops:
  7.2 68.9 %copy-start = (bf16[768,1536]{1,0:T(8,128)(2,1)S(1)}, bf16[768,1536]{1,0:T(8,128)(2,1)}, u32[]{:S(2)}) copy-start(bf16[768,1536]{1,0:T(8,128)(2,1)} %param.9) | copy-start | bytes 7077892
  7.2 68.9 %all-gather.3.cloned.1.call-start = ((), (), s32[]{:S(2)}) async-start(), calls=%async_computation.2 | async-start | bytes 1671168 | tf_op jit(solution)/shard_map/all_gather | solution.py:46
  29.9 93.8 %all-gather.5.cloned.1.call-start = ((), (), s32[]{:S(2)}) async-start(), calls=%async_computation.4 | async-start | bytes 1671168 | tf_op jit(solution)/shard_map/all_gather | solution.py:60
  30.6 363.0 %all-reduce.6.cloned.1.call-start = ((), (), s32[]{:S(2)}) async-start(), calls=%async_computation.6 | async-start | bytes 25165824 | tf_op jit(solution)/shard_map/psum | solution.py:48
  131.0 262.6 %copy-start.6 = (f32[1536]{0:T(1024)S(1)}, f32[1536]{0:T(1024)}, u32[]{:S(2)}) copy-start(f32[1536]{0:T(1024)} %param.10) | copy-start | bytes 18436
  131.0 352.5 %reduce-scatter.5.cloned.1.call-start = ((), (), s32[]{:S(2)}) async-start(), calls=%async_computation.5 | async-start | bytes 3342336 | tf_op jit(solution)/shard_map/reduce_scatter | solution.py:68
  402.8 1.7 copy-start.1
  408.8 153.1 %reduce-scatter.3.cloned.1.call-start = ((), (), s32[]{:S(2)}) async-start(), calls=%async_computation.3 | async-start | bytes 3342336 | tf_op jit(solution)/shard_map/reduce_scatter | solution.py:52
  415.8 0.9 copy-start.4
  416.7 7.5 %copy-start.2 = (bf16[1024,1536]{1,0:T(8,128)(2,1)S(1)}, bf16[1024,1536]{1,0:T(8,128)(2,1)}, u32[]{:S(2)}) copy-start(bf16[1024,1536]{1,0:T(8,128)(2,1)} %get-tuple-element.22) | copy-start | bytes 9437188
  416.7 7.5 %copy-start.8 = (bf16[1024,768]{1,0:T(8,128)(2,1)S(1)}, bf16[1024,768]{1,0:T(8,128)(2,1)}, u32[]{:S(2)}) copy-start(bf16[1024,768]{1,0:T(8,128)(2,1)} %all-gather.5.cloned.1.call-done) | copy-start | bytes 4718596
  424.2 59.3 %copy-start.3 = (bf16[64,768]{1,0:T(8,128)(2,1)S(1)}, bf16[64,768]{1,0:T(8,128)(2,1)}, u32[]{:S(2)}) copy-start(bf16[64,768]{1,0:T(8,128)(2,1)} %param.7) | copy-start | bytes 294916
  424.2 59.3 %copy-start.5 = (f32[768]{0:T(1024)S(1)}, f32[768]{0:T(1024)}, u32[]{:S(2)}) copy-start(f32[768]{0:T(1024)} %param.8) | copy-start | bytes 9220
  424.2 137.7 %copy-start.7 = (f32[768]{0:T(1024)S(1)}, f32[768]{0:T(1024)}, u32[]{:S(2)}) copy-start(f32[768]{0:T(1024)} %param.12) | copy-start | bytes 9220
Sparse Core Ops, SparseCore 0:
  30.0 45.9 all-gather.2
  78.5 45.0 all-gather.4
  131.2 262.3 all-reduce.5
  408.9 74.5 reduce-scatter.4
  487.4 74.4 reduce-scatter.2
where the time goes:
time: 570 us
  waiting for transfers between devices  427 us (75%)
  blocking collectives  73.1 us (13%)
  matrix products  36.4 us (6%)
  other arithmetic  16.4 us (3%)
  between operations  13.8 us (2%)
    psum x1, waiting for transfers between devices, shards(): hidden = lax.psum(partial_value, 'gx') + bias_up  263 us
    reduce_scatter x1, waiting for transfers between devices, shards(): lax.psum_scatter(over_cols(block, w_up), 'gy', scatter_dimension=0, tiled...  54.9 us
    all_gather x1, waiting for transfers between devices, shards(): lax.all_gather(normed, 'gy', axis=0, tiled=True)  45.4 us
    all_gather x1, waiting for transfers between devices, shards(): piece = lax.all_gather(cotangent, 'gy', axis=0, tiled=True)  41.7 us
    psum x1, blocking collectives, shards(): lax.psum((jnp.sum(grad_normed * standard, axis=0), jnp.sum(cotangent, axi...  34.6 us
    reduce_scatter x1, waiting for transfers between devices, shards(): lax.psum_scatter(jnp.dot(block, w_down, preferred_element_type=jnp.float3...  22.2 us
    psum x1, blocking collectives, shards(): lax.psum((jnp.sum(values, axis=1), jnp.sum(values * values, axis=1)), 'gx')  19.8 us
    psum x1, blocking collectives, shards(): lax.psum((jnp.sum(scaled, axis=1), jnp.sum(scaled * standard, axis=1)), '...  18.7 us
  transfers between devices with their start and end apart: 5, of which 5 were waited for; matrix products, arithmetic and copies ran while one was open for 5% of the time, Pallas kernels for 0%

commit v1 on v0

--- a/solution.py
+++ b/solution.py
@@ -57,7 +57,9 @@
         )
         + bias_down
     ).astype(jnp.bfloat16)
-    piece = lax.all_gather(cotangent, "gy", axis=0, tiled=True)
+    piece = jnp.concatenate(
+        lax.all_to_all(jnp.stack([cotangent] * lax.axis_size("gy")), "gy", 0, 0), axis=0
+    )
     weight_total = over_rows(act_whole, piece)
     act_grads = over_cols(piece, w_down)
     grad_act = lax.psum(act_grads, "gx")

time: 570 us -> 526 us (0.923)
  waiting for transfers between devices: 427 us -> 352 us
  blocking collectives: 73.1 us -> 105 us
    all_gather x1 -> x0, waiting for transfers between devices: 41.7 us -> none  [shards(): piece = lax.all_gather(cotangent, 'gy', axis=0, tiled=True)]
    all_gather x1, waiting for transfers between devices: 45.4 us -> 12 us  [shards(): lax.all_gather(normed, 'gy', axis=0, tiled=True)]
    all_to_all x0 -> x1, blocking collectives: none -> 32.2 us  [shards(): lax.all_to_all(jnp.stack([cotangent] * lax.axis_size('gy')), 'gy', 0, 0)]
  transfers between devices with their start and end apart: 5 -> 4, of which waited for: 5 -> 4; matrix products, arithmetic and copies ran while one was open for 5% -> 5% of each run, Pallas kernels for 0% -> 0%
where the time goes in v1:
time: 526 us
  waiting for transfers between devices  352 us (67%)
  blocking collectives  105 us (20%)
  matrix products  33.6 us (6%)
  other arithmetic  16.4 us (3%)
  between operations  13.8 us (3%)
    psum x1, waiting for transfers between devices, shards(): hidden = lax.psum(partial_value, 'gx') + bias_up  263 us
    reduce_scatter x1, waiting for transfers between devices, shards(): lax.psum_scatter(over_cols(block, w_up), 'gy', scatter_dimension=0, tiled...  54.9 us
    psum x1, blocking collectives, shards(): lax.psum((jnp.sum(grad_normed * standard, axis=0), jnp.sum(cotangent, axi...  34.7 us
    all_to_all x1, blocking collectives, shards(): lax.all_to_all(jnp.stack([cotangent] * lax.axis_size('gy')), 'gy', 0, 0)  32.2 us
    reduce_scatter x1, waiting for transfers between devices, shards(): lax.psum_scatter(jnp.dot(block, w_down, preferred_element_type=jnp.float3...  22.2 us
    psum x1, blocking collectives, shards(): lax.psum((jnp.sum(values, axis=1), jnp.sum(values * values, axis=1)), 'gx')  19.8 us
    psum x1, blocking collectives, shards(): lax.psum((jnp.sum(scaled, axis=1), jnp.sum(scaled * standard, axis=1)), '...  18.6 us
    all_gather x1, waiting for transfers between devices, shards(): lax.all_gather(normed, 'gy', axis=0, tiled=True)  12 us
  transfers between devices with their start and end apart: 4, of which 4 were waited for; matrix products, arithmetic and copies ran while one was open for 5% of the time, Pallas kernels for 0%

profile of v1, /device:TPU:0, one launch (start us, length us, event | category | flops | bytes accessed | tf_op | source)
XLA Modules:
  0.0 526.0 jit_solution(10094747155016652233)
XLA Ops:
  7.2 0.0 all-gather.2.cloned.1.call-start
  7.2 1.2 convert_reduce_fusion.1
  8.4 19.8 %all-reduce.2 = (f32[64]{0:T(128)S(1)}, f32[64]{0:T(128)S(1)}) all-reduce(f32[64]{0:T(128)S(1)} %get-tuple-element.11, f32[64]{0:T(128)S(1)} %get-tuple-element.10), channel_id=1, replica_groups=mesh['gx'=8,'gy'=16] {'gx'}, use_global_device_ids=true, to_apply=%region_3.0 | all-reduce | flops 128 | bytes 1024 | tf_op jit(solution)/shard_map/psum | solution.py:37
  28.2 1.6 fusion.11
  29.8 0.0 all-gather.2.cloned.1.call-update
  29.9 0.0 all-reduce.6.cloned.1.call-start
  29.9 1.2 stack.2
  31.1 32.2 %all_to_all.5 = bf16[16,64,768]{2,1,0:T(8,128)(2,1)S(1)} all-to-all(bf16[16,64,768]{2,1,0:T(8,128)(2,1)S(1)} %stack.2), channel_id=1, replica_groups=mesh['gx'=8,'gy'=16] {'gy'}, dimensions={0} | all-to-all | bytes 3145728 | tf_op jit(solution)/shard_map/all_to_all | solution.py:61
  63.3 1.1 copy-done.4
  64.5 4.6 fusion.21
  69.1 12.0 %all-gather.2.cloned.1.call-done = bf16[1024,768]{1,0:T(8,128)(2,1)} async-done(((bf16[64,768]{1,0:T(8,128)(2,1)}), bf16[1024,768]{1,0:T(8,128)(2,1)}) %all-gather.2.cloned.1.call-update) | async-done | bytes 1572880 | tf_op jit(solution)/shard_map/all_gather | solution.py:46
  81.1 5.9 %fusion.19 = f32[1024,1536]{1,0:T(8,128)} fusion(bf16[1024,768]{1,0:T(8,128)(2,1)} %all-gather.2.cloned.1.call-done, bf16[768,1536]{1,0:T(8,128)(2,1)S(1)} %copy-done), kind=kOutput, calls=%fused_computation.32 | convolution fusion | flops 2415919104 | bytes 10223616 | tf_op jit(solution)/shard_map/dot_general | solution.py:45
  87.0 0.0 all-reduce.6.cloned.1.call-update
  87.1 0.0 reduce-scatter.5.cloned.1.call-start
  87.1 262.5 %all-reduce.6.cloned.1.call-done = (f32[1024,1536]{1,0:T(8,128)}, f32[1024,1536]{1,0:T(8,128)}) async-done(((f32[1024,1536]{1,0:T(8,128)}, f32[1024,1536]{1,0:T(8,128)}), (f32[1024,1536]{1,0:T(8,128)}, f32[1024,1536]{1,0:T(8,128)})) %all-reduce.6.cloned.1.call-update) | async-done | bytes 12582928 | tf_op jit(solution)/shard_map/psum | solution.py:48
  349.6 9.2 %convert_reduce_fusion = (f32[1536]{0:T(1024)}, bf16[1024,1536]{1,0:T(8,128)(2,1)S(1)}, bf16[1024,1536]{1,0:T(8,128)(2,1)}) fusion(f32[1024,1536]{1,0:T(8,128)} %get-tuple-element.19, f32[1024,1536]{1,0:T(8,128)} %get-tuple-element.18, f32[1536]{0:T(1024)S(1)} %copy-done.8), kind=kLoop, calls=%fused_computation.7 | loop fusion | flops 25164288 | bytes 18886656 | tf_op jit(solution)/shard_map/reduce_sum | solution.py:67
  358.8 1.7 copy-done.1
  360.5 4.3 fusion.22
  364.8 0.0 reduce-scatter.5.cloned.1.call-update
  364.8 0.0 reduce-scatter.3.cloned.1.call-start
  364.9 6.9 %fusion.20 = f32[1024,768]{1,0:T(8,128)} fusion(bf16[1024,1536]{1,0:T(8,128)(2,1)} %get-tuple-element.22, bf16[1536,768]{1,0:T(8,128)(2,1)} %param.11), kind=kOutput, calls=%fused_computation.33 | convolution fusion | flops 2415919104 | bytes 8650752 | tf_op jit(solution)/shard_map/dot_general | solution.py:53
  371.8 0.0 reduce-scatter.3.cloned.1.call-update
  371.8 0.9 copy-done.6
  372.7 7.5 %fusion.24 = f32[1536,768]{1,0:T(8,128)} fusion(bf16[1024,1536]{1,0:T(8,128)(2,1)} %get-tuple-element.22, bf16[1024,768]{1,0:T(8,128)(2,1)} %bitcast.14), kind=kOutput, calls=%fused_computation.37 | convolution fusion | flops 2415919104 | bytes 9437184 | tf_op jit(solution)/shard_map/dot_general | solution.py:24
  380.3 4.4 fusion.23
  384.7 54.9 %reduce-scatter.5.cloned.1.call-done = f32[64,768]{1,0:T(8,128)} async-done(((f32[1024,768]{1,0:T(8,128)}), f32[64,768]{1,0:T(8,128)}) %reduce-scatter.5.cloned.1.call-update) | async-done | bytes 196624 | tf_op jit(solution)/shard_map/reduce_scatter | solution.py:70
  439.5 1.2 fusion.16
  440.7 18.6 %all-reduce.1 = (f32[64]{0:T(128)S(1)}, f32[64]{0:T(128)S(1)}) all-reduce(f32[64]{0:T(128)S(1)} %get-tuple-element.8, f32[64]{0:T(128)S(1)} %get-tuple-element.9), channel_id=1, replica_groups=mesh['gx'=8,'gy'=16] {'gx'}, use_global_device_ids=true, to_apply=%region_11.0 | all-reduce | flops 128 | bytes 1024 | tf_op jit(solution)/shard_map/psum | solution.py:76
  459.3 34.7 %all-reduce = (f32[768]{0:T(1024)}, f32[768]{0:T(1024)}) all-reduce(f32[768]{0:T(1024)S(1)} %get-tuple-element.7, f32[768]{0:T(1024)S(1)} %convert_reduce_fusion.2), channel_id=1, replica_groups=mesh['gx'=8,'gy'=16] {'gy'}, use_global_device_ids=true, to_apply=%region_13.0 | all-reduce | flops 1536 | bytes 12288 | tf_op jit(solution)/shard_map/psum | solution.py:71
  494.0 1.7 fusion.15
  495.7 22.2 %reduce-scatter.3.cloned.1.call-done = f32[64,768]{1,0:T(8,128)} async-done(((f32[1024,768]{1,0:T(8,128)}), f32[64,768]{1,0:T(8,128)}) %reduce-scatter.3.cloned.1.call-update) | async-done | bytes 196624 | tf_op jit(solution)/shard_map/reduce_scatter | solution.py:52
  517.9 1.6 add_convert_fusion
  (22 shorter events, 0.1 us)
Async XLA Ops:
  7.2 74.0 %copy-start = (bf16[768,1536]{1,0:T(8,128)(2,1)S(1)}, bf16[768,1536]{1,0:T(8,128)(2,1)}, u32[]{:S(2)}) copy-start(bf16[768,1536]{1,0:T(8,128)(2,1)} %param.9) | copy-start | bytes 7077892
  7.2 74.0 %all-gather.2.cloned.1.call-start = ((), (), s32[]{:S(2)}) async-start(), calls=%async_computation.3 | async-start | bytes 1671168 | tf_op jit(solution)/shard_map/all_gather | solution.py:46
  29.9 319.7 %all-reduce.6.cloned.1.call-start = ((), (), s32[]{:S(2)}) async-start(), calls=%async_computation.6 | async-start | bytes 25165824 | tf_op jit(solution)/shard_map/psum | solution.py:48
  29.9 34.6 %copy-start.10 = (bf16[1536,768]{1,0:T(8,128)(2,1)S(1)}, bf16[1536,768]{1,0:T(8,128)(2,1)}, u32[]{:S(2)}) copy-start(bf16[1536,768]{1,0:T(8,128)(2,1)} %param.11) | copy-start | bytes 7077892
  63.3 1.1 copy-start.4
  87.0 262.6 %copy-start.8 = (f32[1536]{0:T(1024)S(1)}, f32[1536]{0:T(1024)}, u32[]{:S(2)}) copy-start(f32[1536]{0:T(1024)} %param.10) | copy-start | bytes 18436
  87.1 352.5 %reduce-scatter.5.cloned.1.call-start = ((), (), s32[]{:S(2)}) async-start(), calls=%async_computation.5 | async-start | bytes 3342336 | tf_op jit(solution)/shard_map/reduce_scatter | solution.py:70
  358.8 1.7 copy-start.1
  364.8 153.1 %reduce-scatter.3.cloned.1.call-start = ((), (), s32[]{:S(2)}) async-start(), calls=%async_computation.4 | async-start | bytes 3342336 | tf_op jit(solution)/shard_map/reduce_scatter | solution.py:52
  371.8 0.9 copy-start.6
  372.7 7.6 %copy-start.2 = (bf16[1024,1536]{1,0:T(8,128)(2,1)S(1)}, bf16[1024,1536]{1,0:T(8,128)(2,1)}, u32[]{:S(2)}) copy-start(bf16[1024,1536]{1,0:T(8,128)(2,1)} %copy-done.1) | copy-start | bytes 9437188
  372.7 7.5 %copy-start.3 = (bf16[1024,768]{1,0:T(8,128)(2,1)S(1)}, bf16[1024,768]{1,0:T(8,128)(2,1)}, u32[]{:S(2)}) copy-start(bf16[1024,768]{1,0:T(8,128)(2,1)} %all-gather.2.cloned.1.call-done) | copy-start | bytes 4718596
  380.3 59.3 %copy-start.5 = (bf16[64,768]{1,0:T(8,128)(2,1)S(1)}, bf16[64,768]{1,0:T(8,128)(2,1)}, u32[]{:S(2)}) copy-start(bf16[64,768]{1,0:T(8,128)(2,1)} %param.7) | copy-start | bytes 294916
  380.3 59.3 %copy-start.7 = (f32[768]{0:T(1024)S(1)}, f32[768]{0:T(1024)}, u32[]{:S(2)}) copy-start(f32[768]{0:T(1024)} %param.8) | copy-start | bytes 9220
  380.3 137.6 %copy-start.9 = (f32[768]{0:T(1024)S(1)}, f32[768]{0:T(1024)}, u32[]{:S(2)}) copy-start(f32[768]{0:T(1024)} %param.12) | copy-start | bytes 9220
Sparse Core Ops, SparseCore 0:
  30.0 51.1 all-gather.1
  87.2 262.3 all-reduce.5
  365.0 74.5 reduce-scatter.4
  443.4 74.4 reduce-scatter.2
